TPU v7x, 32 devices: a whole 2x2x4 slice. The times are simulated.
32 devices in a mesh: row: 8 (over z, core), col: 4 (over y, x).
Axes of the slice: x: 2, y: 2, z: 4, core: 2. Of those that a mesh axis runs over, the one named last changes fastest.
Arguments:
- affinity: float32 [16384, 16384], P('row', 'col'), as said below
Outputs:
- reduced: float32 [16384, 16384], P('row', 'col')
Inputs may be any that keep to these rules, and one draw needn't show every extreme that they name: The matrix that affinity stores is exactly symmetric in global indexing.
All inputs are finite; a program needn't handle non-finite values.
Results may differ from a plain program's by a relative error of at most 0.0003.
Values sent between devices are 32-bit elements; how exact they have to be, the bound alone decides.
No kernel may reach another device: no remote copies, remote signals or barrier semaphores. Data moves between devices by JAX's collectives and lax.ppermute only.
A program may use at most 192 MiB of HBM per device.

v0:
```python
import jax
import jax.numpy as jnp
from jax import lax
from jax.sharding import PartitionSpec as P

B = 256
PANELS = 2
NS_STEPS = 12
PRECISE = lax.Precision.HIGHEST


def spread(block, axis, owner):
    block = jnp.where(lax.axis_index(axis) == owner, block, jnp.zeros_like(block))
    return lax.psum(block, axis)


def matmul(first_op, second_op, first_dim, second_dim):
    return lax.dot_general(
        first_op,
        second_op,
        (((first_dim,), (second_dim,)), ((), ())),
        precision=PRECISE,
        preferred_element_type=jnp.float32,
    )


def lower_inverse(square):
    lower_factor = jnp.linalg.cholesky(square)
    identity = jnp.eye(square.shape[0], dtype=jnp.float32)
    return lax.linalg.triangular_solve(lower_factor, identity, left_side=True, lower=True)


def reflector_parts(gram_matrix, top_block):
    inverse_low = lower_inverse(gram_matrix)
    top_basis = matmul(top_block, inverse_low, 1, 1)
    polar_part = top_basis
    for repeat in range(NS_STEPS):
        polar_part = 1.5 * polar_part - 0.5 * matmul(
            polar_part, matmul(polar_part, polar_part, 0, 0), 1, 0
        )
    cross_term = matmul(polar_part, top_basis, 0, 0)
    identity = jnp.eye(gram_matrix.shape[0], dtype=jnp.float32)
    metric = identity + cross_term + cross_term.T + matmul(polar_part, polar_part, 0, 0)
    metric_inv = lower_inverse(metric)
    middle = 2.0 * matmul(metric_inv, metric_inv, 0, 0)
    return (inverse_low, polar_part, middle)


def body(affinity):
    rows_here = affinity.shape[0]
    cols_here = affinity.shape[1]
    row_count = lax.axis_size("row")
    col_count = lax.axis_size("col")
    row_rank = lax.axis_index("row")
    col_rank = lax.axis_index("col")
    fold_count = row_count // col_count
    row_blocks = jnp.arange(rows_here, dtype=jnp.int32) // B * row_count + row_rank
    matrix = affinity

    def to_columns(row_panel):
        pieces = []
        for part_num in range(fold_count):
            pieces.append(spread(row_panel, "row", col_rank + part_num * col_count))
        stacked = jnp.stack(pieces).reshape(fold_count, rows_here // B, B, B)
        return jnp.transpose(stacked, (3, 1, 0, 2)).reshape(B, cols_here)

    for panel_num in range(PANELS):
        col_start = panel_num // col_count * B
        owned_cols = matrix[:, col_start : col_start + B]
        panel_rows = spread(owned_cols, "col", panel_num % col_count)
        panel_rows = jnp.where((row_blocks > panel_num)[:, None], panel_rows, 0.0)
        top_start = (panel_num + 1) // row_count * B
        top_mask = (row_rank == (panel_num + 1) % row_count).astype(jnp.float32)
        top_piece = top_mask * panel_rows[top_start : top_start + B]
        gram_matrix, top_block = lax.psum((matmul(panel_rows, panel_rows, 0, 0), top_piece), "row")
        inverse_low, polar_part, middle = reflector_parts(gram_matrix, top_block)
        reflect_rows = (
            matmul(panel_rows, inverse_low, 1, 1)
            .at[top_start : top_start + B]
            .add(top_mask * polar_part)
        )
        reflect_cols = to_columns(reflect_rows)
        local_product = matmul(matrix, reflect_cols, 1, 1)
        product_rows = lax.psum(local_product, "col")
        image_rows = matmul(product_rows, middle, 1, 0)
        coupling = lax.psum(matmul(reflect_rows, image_rows, 0, 0), "row")
        shift_term = matmul(middle, coupling, 1, 0)
        companion_rows = image_rows - 0.5 * matmul(reflect_rows, shift_term, 1, 0)
        companion_cols = to_columns(companion_rows)
        matrix = matrix - matmul(
            jnp.concatenate((reflect_rows, companion_rows), 1),
            jnp.concatenate((companion_cols, reflect_cols), 0),
            1,
            0,
        )
    return matrix


def solution(mesh):
    return jax.shard_map(
        body, mesh=mesh, in_specs=(P("row", "col"),), out_specs=P("row", "col"), check_vma=False
    )
```

profile of v0, /device:TPU:0, one launch (start us, length us, event | category | flops | bytes accessed | tf_op | source)
XLA Modules:
  0.0 1348.9 jit_solution(7293248256234329230)
XLA Ops:
  6.5 3.0 slice_select_fusion.1
  9.7 73.0 %all-reduce.20.cloned.1.call-done = f32[2048,256]{1,0:T(8,128)} async-done(((f32[2048,256]{1,0:T(8,128)}), f32[2048,256]{1,0:T(8,128)}) %all-reduce.20.cloned.1.call-update) | async-done | bytes 2097168 | tf_op jit(solution)/shard_map/psum | solution.py:14
  84.6 4.3 fusion.102
  89.9 56.5 %all-reduce.42.cloned.1.call-done = (f32[256,256]{0,1:T(8,128)}, f32[256,256]{1,0:T(8,128)}) async-done(((f32[256,256]{0,1:T(8,128)}, f32[256,256]{1,0:T(8,128)}), (f32[256,256]{0,1:T(8,128)}, f32[256,256]{1,0:T(8,128)})) %all-reduce.42.cloned.1.call-update) | async-done | bytes 524304 | tf_op jit(solution)/shard_map/psum | solution.py:75
  148.5 11.7 cholesky.214
  160.3 9.8 custom-call.17
  170.6 11.7 cholesky.231
  184.4 4.1 while.10
  188.5 19.9 %custom-call.18 = f32[2,128,128]{1,2,0:T(8,128)S(1)} custom-call(f32[2,128,128]{2,1,0:T(8,128)S(1)} %get-tuple-element.57), custom_call_target="InvertDiagBlocksLowerTriangular" | custom-call | tf_op jit(solution)/shard_map/triangular_solve/custom-call.0 | solution.py:30
  209.4 3.5 fusion.54
  229.7 11.7 cholesky.248
  241.5 9.8 custom-call.19
  251.8 72.1 %all-reduce.40.cloned.1.call-done = (f32[1,8,256,256]{3,2,0,1:T(8,128)}, f32[1,8,256,256]{3,2,0,1:T(8,128)}) async-done(((f32[1,8,256,256]{3,2,0,1:T(8,128)}, f32[1,8,256,256]{3,2,0,1:T(8,128)}), (f32[1,8,256,256]{3,2,0,1:T(8,128)}, f32[1,8,256,256]{3,2,0,1:T(8,128)})) %all-reduce.40.cloned.1.call-update) | async-done | bytes 4194320 | tf_op jit(solution)/shard_map/psum | solution.py:14
  328.6 58.3 %convolution_bitcast_fusion = f32[2048,256]{0,1:T(8,128)} fusion(f32[256,4096]{0,1:T(8,128)S(1)} %bitcast.302, f32[2048,4096]{1,0:T(8,128)} %param.8), kind=kOutput, calls=%fused_computation.30 | convolution fusion | flops 25769803776 | bytes 39845888 | tf_op jit(solution)/shard_map/dot_general | solution.py:18
  387.7 11.7 cholesky.265
  401.4 3.9 while.11
  405.3 19.7 %custom-call.20 = f32[2,128,128]{1,2,0:T(8,128)S(1)} custom-call(f32[2,128,128]{2,1,0:T(8,128)S(1)} %get-tuple-element.58), custom_call_target="InvertDiagBlocksLowerTriangular" | custom-call | tf_op jit(solution)/shard_map/triangular_solve/custom-call.0 | solution.py:30
  426.6 30.3 %all-reduce.22.cloned.1.call-done = f32[2048,256]{0,1:T(8,128)} async-done(((f32[2048,256]{0,1:T(8,128)}), f32[2048,256]{0,1:T(8,128)}) %all-reduce.22.cloned.1.call-update) | async-done | bytes 2097168 | tf_op jit(solution)/shard_map/psum | solution.py:84
  456.9 5.2 fusion.116
  463.4 4.2 fusion.117
  467.9 55.3 %all-reduce.24.cloned.1.call-done = f32[256,256]{1,0:T(8,128)} async-done(((f32[256,256]{1,0:T(8,128)}), f32[256,256]{1,0:T(8,128)}) %all-reduce.24.cloned.1.call-update) | async-done | bytes 262160 | tf_op jit(solution)/shard_map/psum | solution.py:86
  524.6 6.0 broadcast_select_fusion.6
  530.7 95.7 %all-reduce.38.cloned.1.call-done = (f32[1,8,256,256]{3,2,0,1:T(8,128)}, f32[1,8,256,256]{3,2,0,1:T(8,128)}) async-done(((f32[1,8,256,256]{3,2,0,1:T(8,128)}, f32[1,8,256,256]{3,2,0,1:T(8,128)}), (f32[1,8,256,256]{3,2,0,1:T(8,128)}, f32[1,8,256,256]{3,2,0,1:T(8,128)})) %all-reduce.38.cloned.1.call-update) | async-done | bytes 4194320 | tf_op jit(solution)/shard_map/psum | solution.py:14
  630.5 59.6 %convolution_subtract_fusion.1 = f32[2048,4096]{1,0:T(8,128)} fusion(f32[2048,4096]{1,0:T(8,128)} %param.8, f32[256,4096]{0,1:T(8,128)S(1)} %bitcast.303, f32[256,4096]{0,1:T(8,128)S(1)} %bitcast.307, f32[2048,256]{1,0:T(8,128)S(1)} %copy-done.8, f32[2048,256]{1,0:T(8,128)S(1)} %get-tuple-element.139), kind=kOutput, calls=%fused_computation.9 | convolution fusion | flops 51551141888 | bytes 79691776 | tf_op jit(solution)/shard_map/dot_general | solution.py:18
  690.0 3.0 slice_select_fusion
  693.1 69.6 %all-reduce.26.cloned.1.call-done = f32[2048,256]{1,0:T(8,128)} async-done(((f32[2048,256]{1,0:T(8,128)}), f32[2048,256]{1,0:T(8,128)}) %all-reduce.26.cloned.1.call-update) | async-done | bytes 2097168 | tf_op jit(solution)/shard_map/psum | solution.py:14
  764.7 4.3 fusion.119
  770.2 56.3 %all-reduce.36.cloned.1.call-done = (f32[256,256]{0,1:T(8,128)}, f32[256,256]{1,0:T(8,128)}) async-done(((f32[256,256]{0,1:T(8,128)}, f32[256,256]{1,0:T(8,128)}), (f32[256,256]{0,1:T(8,128)}, f32[256,256]{1,0:T(8,128)})) %all-reduce.36.cloned.1.call-update) | async-done | bytes 524304 | tf_op jit(solution)/shard_map/psum | solution.py:75
  828.6 11.7 cholesky.282
  841.1 9.8 custom-call.21
  851.4 11.7 cholesky.299
  865.1 4.0 while.12
  869.1 19.8 %custom-call.22 = f32[2,128,128]{1,2,0:T(8,128)S(1)} custom-call(f32[2,128,128]{2,1,0:T(8,128)S(1)} %get-tuple-element.59), custom_call_target="InvertDiagBlocksLowerTriangular" | custom-call | tf_op jit(solution)/shard_map/triangular_solve/custom-call.0 | solution.py:30
  890.0 3.5 fusion.52
  910.0 11.7 cholesky.316
  921.8 9.8 custom-call.23
  932.1 72.1 %all-reduce.34.cloned.1.call-done = (f32[1,8,256,256]{3,2,0,1:T(8,128)}, f32[1,8,256,256]{3,2,0,1:T(8,128)}) async-done(((f32[1,8,256,256]{3,2,0,1:T(8,128)}, f32[1,8,256,256]{3,2,0,1:T(8,128)}), (f32[1,8,256,256]{3,2,0,1:T(8,128)}, f32[1,8,256,256]{3,2,0,1:T(8,128)})) %all-reduce.34.cloned.1.call-update) | async-done | bytes 4194320 | tf_op jit(solution)/shard_map/psum | solution.py:14
  1008.9 31.4 %fusion.132 = f32[2048,256]{1,0:T(8,128)} fusion(f32[2048,4096]{1,0:T(8,128)} %convolution_subtract_fusion.1, f32[256,4096]{0,1:T(8,128)S(1)} %bitcast.304), kind=kOutput, calls=%fused_computation.258 | convolution fusion | flops 25769803776 | bytes 39845888 | tf_op jit(solution)/shard_map/dot_general | solution.py:18
  1041.0 11.7 cholesky.333
  1054.7 4.0 while.13
  1058.7 19.7 %custom-call.24 = f32[2,128,128]{1,2,0:T(8,128)S(1)} custom-call(f32[2,128,128]{2,1,0:T(8,128)S(1)} %get-tuple-element.60), custom_call_target="InvertDiagBlocksLowerTriangular" | custom-call | tf_op jit(solution)/shard_map/triangular_solve/custom-call.0 | solution.py:30
  1080.0 30.1 %all-reduce.28.cloned.1.call-done = f32[2048,256]{1,0:T(8,128)} async-done(((f32[2048,256]{1,0:T(8,128)}), f32[2048,256]{1,0:T(8,128)}) %all-reduce.28.cloned.1.call-update) | async-done | bytes 2097168 | tf_op jit(solution)/shard_map/psum | solution.py:84
  1110.2 3.5 fusion.134
  1115.0 4.2 fusion.135
  1119.3 55.5 %all-reduce.30.cloned.1.call-done = f32[256,256]{1,0:T(8,128)} async-done(((f32[256,256]{1,0:T(8,128)}), f32[256,256]{1,0:T(8,128)}) %all-reduce.30.cloned.1.call-update) | async-done | bytes 262160 | tf_op jit(solution)/shard_map/psum | solution.py:86
  1176.1 6.1 broadcast_select_fusion.1
  1182.2 95.7 %all-reduce.32.cloned.1.call-done = (f32[1,8,256,256]{3,2,0,1:T(8,128)}, f32[1,8,256,256]{3,2,0,1:T(8,128)}) async-done(((f32[1,8,256,256]{3,2,0,1:T(8,128)}, f32[1,8,256,256]{3,2,0,1:T(8,128)}), (f32[1,8,256,256]{3,2,0,1:T(8,128)}, f32[1,8,256,256]{3,2,0,1:T(8,128)})) %all-reduce.32.cloned.1.call-update) | async-done | bytes 4194320 | tf_op jit(solution)/shard_map/psum | solution.py:14
  1282.1 59.7 %convolution_subtract_fusion = f32[2048,4096]{1,0:T(8,128)} fusion(f32[2048,4096]{1,0:T(8,128)} %convolution_subtract_fusion.1, f32[256,4096]{0,1:T(8,128)S(1)} %bitcast.305, f32[256,4096]{0,1:T(8,128)S(1)} %bitcast.306, f32[2048,256]{1,0:T(8,128)S(1)} %copy-done.9, f32[2048,256]{1,0:T(8,128)S(1)} %get-tuple-element.146), kind=kOutput, calls=%fused_computation.8 | convolution fusion | flops 51551141888 | bytes 79691776 | tf_op jit(solution)/shard_map/dot_general | solution.py:18
  (206 shorter events, 94.4 us)
Async XLA Ops:
  6.5 76.1 %all-reduce.20.cloned.1.call-start = ((), (), s32[]{:S(2)}) async-start(), calls=%async_computation | async-start | bytes 4194304 | tf_op jit(solution)/shard_map/psum | solution.py:14
  9.6 136.8 %all-reduce.42.cloned.1.call-start = ((), (), s32[]{:S(2)}) async-start(), calls=%async_computation.11 | async-start | bytes 1048576 | tf_op jit(solution)/shard_map/psum | solution.py:75
  84.6 4.3 copy-start.4
  89.6 234.3 %all-reduce.40.cloned.1.call-start = ((), (), s32[]{:S(2)}) async-start(), calls=%async_computation.10 | async-start | bytes 8388608 | tf_op jit(solution)/shard_map/psum | solution.py:14
  209.4 3.5 copy-start.10
  228.1 228.8 %all-reduce.22.cloned.1.call-start = ((), (), s32[]{:S(2)}) async-start(), calls=%async_computation.1 | async-start | bytes 4194304 | tf_op jit(solution)/shard_map/psum | solution.py:84
  326.6 2.0 copy-start
  387.0 136.2 %all-reduce.24.cloned.1.call-start = ((), (), s32[]{:S(2)}) async-start(), calls=%async_computation.2 | async-start | bytes 524288 | tf_op jit(solution)/shard_map/psum | solution.py:86
  462.1 1.3 copy-start.7
  467.6 158.7 %all-reduce.38.cloned.1.call-start = ((), (), s32[]{:S(2)}) async-start(), calls=%async_computation.9 | async-start | bytes 8388608 | tf_op jit(solution)/shard_map/psum | solution.py:14
  530.6 232.1 %all-reduce.26.cloned.1.call-start = ((), (), s32[]{:S(2)}) async-start(), calls=%async_computation.3 | async-start | bytes 4194304 | tf_op jit(solution)/shard_map/psum | solution.py:14
  626.3 3.4 copy-start.1
  626.3 4.1 copy-start.8
  693.1 133.5 %all-reduce.36.cloned.1.call-start = ((), (), s32[]{:S(2)}) async-start(), calls=%async_computation.8 | async-start | bytes 1048576 | tf_op jit(solution)/shard_map/psum | solution.py:75
  764.7 4.3 copy-start.5
  769.8 234.5 %all-reduce.34.cloned.1.call-start = ((), (), s32[]{:S(2)}) async-start(), calls=%async_computation.7 | async-start | bytes 8388608 | tf_op jit(solution)/shard_map/psum | solution.py:14
  890.0 3.5 copy-start.11
  908.4 201.7 %all-reduce.28.cloned.1.call-start = ((), (), s32[]{:S(2)}) async-start(), calls=%async_computation.4 | async-start | bytes 4194304 | tf_op jit(solution)/shard_map/psum | solution.py:84
  1006.9 1.9 copy-start.2
  1040.3 134.5 %all-reduce.30.cloned.1.call-start = ((), (), s32[]{:S(2)}) async-start(), calls=%async_computation.5 | async-start | bytes 524288 | tf_op jit(solution)/shard_map/psum | solution.py:86
  1113.7 1.3 copy-start.6
  1119.2 158.7 %all-reduce.32.cloned.1.call-start = ((), (), s32[]{:S(2)}) async-start(), calls=%async_computation.6 | async-start | bytes 8388608 | tf_op jit(solution)/shard_map/psum | solution.py:14
  1278.0 3.4 copy-start.3
  1278.0 4.1 copy-start.9
Sparse Core Ops, SparseCore 0:
  10.4 72.1 all-reduce.19
  89.8 56.6 all-reduce.41
  228.2 95.6 all-reduce.39
  387.1 69.7 all-reduce.21
  467.8 55.4 all-reduce.23
  530.7 95.5 all-reduce.37
  693.2 69.4 all-reduce.25
  769.9 56.6 all-reduce.35
  908.6 95.6 all-reduce.33
  1040.4 69.6 all-reduce.27
  1119.4 55.4 all-reduce.29
  1182.4 95.5 all-reduce.31
where the time goes:
time: 1350 us
  waiting for transfers between devices  763 us (57%)
  matrix products  291 us (22%)
  other arithmetic  246 us (18%)
  local copies, waits for them, and re-layouts  27.7 us (2%)
  between operations  19.9 us (1%)
    psum x6, waiting for transfers between devices, spread(): return lax.psum(block, axis)  478 us
    dot_general x72, matrix products, matmul(): lax.dot_general(first_op, second_op, (((first_dim,), (second_dim,)), ((),...  285 us
    another operation x27, other arithmetic, lower_inverse(): lower_factor = jnp.linalg.cholesky(square)  138 us
    psum x2, waiting for transfers between devices, body(): lax.psum((matmul(panel_rows, panel_rows, 0, 0), top_piece), 'row')  113 us
    psum x2, waiting for transfers between devices, body(): coupling = lax.psum(matmul(reflect_rows, image_rows, 0, 0), 'row')  111 us
    another operation x9, other arithmetic, lower_inverse(): lax.linalg.triangular_solve(lower_factor, identity, left_side=True, lower...  79.2 us
    psum x2, waiting for transfers between devices, body(): product_rows = lax.psum(local_product, 'col')  60.4 us
  transfers between devices with their start and end apart: 12, of which 12 were waited for; matrix products, arithmetic and copies ran while one was open for 9% of the time, Pallas kernels for 0%

commit v1 on v0

--- a/solution.py
+++ b/solution.py
@@ -11,7 +11,12 @@
 
 def spread(block, axis, owner):
     block = jnp.where(lax.axis_index(axis) == owner, block, jnp.zeros_like(block))
-    return lax.psum(block, axis)
+
+    def update_frame_now(xs):
+        field_out = lax.all_gather(xs, axis)
+        return jnp.sum(field_out, axis=0)
+
+    return update_frame_now(block)
 
 
 def matmul(first_op, second_op, first_dim, second_dim):

time: 1350 us -> 2440 us (1.81)
  waiting for transfers between devices: 763 us -> 1510 us
  local copies, waits for them, and re-layouts: 27.7 us -> 282 us
  other arithmetic: 246 us -> 308 us
    all_gather x0 -> x10, waiting for transfers between devices: none -> 1200 us  [update_frame_now(): field_out = lax.all_gather(xs, axis)]
    psum x6 -> x0, waiting for transfers between devices: 478 us -> none  [spread(): return lax.psum(block, axis)]
    unnamed x24 -> x33, local copies, waits for them, and re-layouts: 9.23 us -> 189 us
    reduce_sum x0 -> x10, other arithmetic: none -> 65.9 us  [update_frame_now(): return jnp.sum(field_out, axis=0)]
    sub x0 -> x1, local copies, waits for them, and re-layouts: none -> 31.1 us  [body(): matrix - matmul(jnp.concatenate((reflect_rows, companion_rows), 1), jnp.c...]
  transfers between devices with their start and end apart: 12 -> 16, of which waited for: 12 -> 16; matrix products, arithmetic and copies ran while one was open for 9% -> 9% of each run, Pallas kernels for 0% -> 0%
where the time goes in v1:
time: 2440 us; the launch traced here: 2430 us
  waiting for transfers between devices  1510 us (62%)
  matrix products  313 us (13%)
  other arithmetic  308 us (13%)
  local copies, waits for them, and re-layouts  282 us (12%)
    all_gather x10, waiting for transfers between devices, update_frame_now(): field_out = lax.all_gather(xs, axis)  1200 us
    dot_general x72, matrix products, matmul(): lax.dot_general(first_op, second_op, (((first_dim,), (second_dim,)), ((),...  307 us
    unnamed x33, local copies, waits for them, and re-layouts  189 us
    another operation x27, other arithmetic, lower_inverse(): lower_factor = jnp.linalg.cholesky(square)  138 us
    psum x2, waiting for transfers between devices, body(): lax.psum((matmul(panel_rows, panel_rows, 0, 0), top_piece), 'row')  113 us
    psum x2, waiting for transfers between devices, body(): coupling = lax.psum(matmul(reflect_rows, image_rows, 0, 0), 'row')  111 us
    psum x2, waiting for transfers between devices, body(): product_rows = lax.psum(local_product, 'col')  80.4 us
    another operation x9, other arithmetic, lower_inverse(): lax.linalg.triangular_solve(lower_factor, identity, left_side=True, lower...  79.4 us
  transfers between devices with their start and end apart: 16, of which 16 were waited for; matrix products, arithmetic and copies ran while one was open for 9% of the time, Pallas kernels for 0%

profile of v1, /device:TPU:0, one launch (start us, length us, event | category | flops | bytes accessed | tf_op | source)
XLA Modules:
  0.0 2433.1 jit_solution(1746692952090603767)
XLA Ops:
  6.5 33.3 %copy.43 = f32[2048,4096]{0,1:T(8,128)} copy(f32[2048,4096]{1,0:T(8,128)} %param.8) | data formatting | bytes 67108864 | tf_op args[0]
  43.2 90.3 %all-gather.21.cloned.1.call-done = f32[8192,256]{0,1:T(8,128)} async-done(((f32[2048,256]{0,1:T(8,128)}), f32[8192,256]{0,1:T(8,128)}) %all-gather.21.cloned.1.call-update) | async-done | bytes 8388624 | tf_op jit(solution)/shard_map/all_gather | solution.py:16
  133.5 10.8 reshape.155
  157.0 56.2 %all-reduce.20.cloned.1.call-done = (f32[256,256]{0,1:T(8,128)}, f32[256,256]{0,1:T(8,128)}) async-done(((f32[256,256]{0,1:T(8,128)}, f32[256,256]{0,1:T(8,128)}), (f32[256,256]{0,1:T(8,128)}, f32[256,256]{0,1:T(8,128)})) %all-reduce.20.cloned.1.call-update) | async-done | bytes 524304 | tf_op jit(solution)/shard_map/psum | solution.py:80
  215.3 11.7 cholesky.214
  227.1 9.8 custom-call.17
  237.4 11.7 cholesky.231
  254.9 19.9 custom-call.18
  297.0 11.7 cholesky.248
  308.8 9.8 custom-call.19
  319.1 11.7 cholesky.265
  330.8 114.8 %all-gather.23.cloned.1.call-done = f32[16384,256]{0,1:T(8,128)} async-done(((f32[2048,256]{0,1:T(8,128)}), f32[16384,256]{0,1:T(8,128)}) %all-gather.23.cloned.1.call-update) | async-done | bytes 16777232 | tf_op jit(solution)/shard_map/all_gather | solution.py:16
  445.5 17.7 copy.71
  472.9 123.4 %all-gather.25.cloned.1.call-done = f32[16384,256]{0,1:T(8,128)} async-done(((f32[2048,256]{0,1:T(8,128)}), f32[16384,256]{0,1:T(8,128)}) %all-gather.25.cloned.1.call-update) | async-done | bytes 16777232 | tf_op jit(solution)/shard_map/all_gather | solution.py:16
  596.3 17.6 copy.72
  628.2 58.4 %convolution_bitcast_fusion = f32[2048,256]{0,1:T(8,128)} fusion(f32[256,4096]{0,1:T(8,128)S(1)} %bitcast.346, f32[2048,4096]{1,0:T(8,128)} %param.8), kind=kOutput, calls=%fused_computation.38 | convolution fusion | flops 25769803776 | bytes 39845888 | tf_op jit(solution)/shard_map/dot_general | solution.py:23
  693.1 19.7 custom-call.20
  714.4 40.2 %all-reduce.10.cloned.1.call-done = f32[2048,256]{0,1:T(8,128)} async-done(((f32[2048,256]{0,1:T(8,128)}), f32[2048,256]{0,1:T(8,128)}) %all-reduce.10.cloned.1.call-update) | async-done | bytes 2097168 | tf_op jit(solution)/shard_map/psum | solution.py:89
  762.3 55.5 %all-reduce.12.cloned.1.call-done = f32[256,256]{1,0:T(8,128)} async-done(((f32[256,256]{1,0:T(8,128)}), f32[256,256]{1,0:T(8,128)}) %all-reduce.12.cloned.1.call-update) | async-done | bytes 262160 | tf_op jit(solution)/shard_map/psum | solution.py:91
  826.6 149.5 %all-gather.27.cloned.1.call-done = f32[16384,256]{0,1:T(8,128)} async-done(((f32[2048,256]{0,1:T(8,128)}), f32[16384,256]{0,1:T(8,128)}) %all-gather.27.cloned.1.call-update) | async-done | bytes 16777232 | tf_op jit(solution)/shard_map/all_gather | solution.py:16
  976.1 17.7 copy.73
  1001.4 125.6 %all-gather.29.cloned.1.call-done = f32[16384,256]{0,1:T(8,128)} async-done(((f32[2048,256]{0,1:T(8,128)}), f32[16384,256]{0,1:T(8,128)}) %all-gather.29.cloned.1.call-update) | async-done | bytes 16777232 | tf_op jit(solution)/shard_map/all_gather | solution.py:16
  1127.0 17.6 copy.75
  1159.3 61.0 %convolution_subtract_fusion.1 = f32[2048,4096]{0,1:T(8,128)} fusion(f32[2048,4096]{0,1:T(8,128)} %copy.43, f32[256,4096]{0,1:T(8,128)} %bitcast.347, f32[256,4096]{0,1:T(8,128)} %bitcast.350, f32[2048,256]{0,1:T(8,128)} %get-tuple-element.135, f32[2048,256]{0,1:T(8,128)S(1)} %get-tuple-element.131), kind=kOutput, calls=%fused_computation.17 | convolution fusion | flops 51551141888 | bytes 79691776 | tf_op jit(solution)/shard_map/dot_general | solution.py:23
  1223.6 85.7 %all-gather.31.cloned.1.call-done = f32[8192,256]{0,1:T(8,128)} async-done(((f32[2048,256]{0,1:T(8,128)}), f32[8192,256]{0,1:T(8,128)}) %all-gather.31.cloned.1.call-update) | async-done | bytes 8388624 | tf_op jit(solution)/shard_map/all_gather | solution.py:16
  1309.4 11.2 reshape.160
  1333.0 56.6 %all-reduce.18.cloned.1.call-done = (f32[256,256]{0,1:T(8,128)}, f32[256,256]{0,1:T(8,128)}) async-done(((f32[256,256]{0,1:T(8,128)}, f32[256,256]{0,1:T(8,128)}), (f32[256,256]{0,1:T(8,128)}, f32[256,256]{0,1:T(8,128)})) %all-reduce.18.cloned.1.call-update) | async-done | bytes 524304 | tf_op jit(solution)/shard_map/psum | solution.py:80
  1391.6 11.7 cholesky.282
  1403.4 9.8 custom-call.21
  1413.7 11.7 cholesky.299
  1431.8 20.1 custom-call.22
  1473.8 11.7 cholesky.316
  1485.6 9.8 custom-call.23
  1495.9 11.7 cholesky.333
  1507.6 114.8 %all-gather.33.cloned.1.call-done = f32[16384,256]{0,1:T(8,128)} async-done(((f32[2048,256]{0,1:T(8,128)}), f32[16384,256]{0,1:T(8,128)}) %all-gather.33.cloned.1.call-update) | async-done | bytes 16777232 | tf_op jit(solution)/shard_map/all_gather | solution.py:16
  1622.4 18.0 copy.77
  1650.0 123.2 %all-gather.35.cloned.1.call-done = f32[16384,256]{0,1:T(8,128)} async-done(((f32[2048,256]{0,1:T(8,128)}), f32[16384,256]{0,1:T(8,128)}) %all-gather.35.cloned.1.call-update) | async-done | bytes 16777232 | tf_op jit(solution)/shard_map/all_gather | solution.py:16
  1773.2 17.6 copy.78
  1805.1 57.1 %fusion.132 = f32[2048,256]{1,0:T(8,128)} fusion(f32[2048,4096]{0,1:T(8,128)} %convolution_subtract_fusion.1, f32[256,4096]{0,1:T(8,128)S(1)} %bitcast.348), kind=kOutput, calls=%fused_computation.266 | convolution fusion | flops 25769803776 | bytes 39845888 | tf_op jit(solution)/shard_map/dot_general | solution.py:23
  1868.6 19.7 custom-call.24
  1889.9 40.2 %all-reduce.14.cloned.1.call-done = f32[2048,256]{1,0:T(8,128)} async-done(((f32[2048,256]{1,0:T(8,128)}), f32[2048,256]{1,0:T(8,128)}) %all-reduce.14.cloned.1.call-update) | async-done | bytes 2097168 | tf_op jit(solution)/shard_map/psum | solution.py:89
  1937.7 55.5 %all-reduce.16.cloned.1.call-done = f32[256,256]{1,0:T(8,128)} async-done(((f32[256,256]{1,0:T(8,128)}), f32[256,256]{1,0:T(8,128)}) %all-reduce.16.cloned.1.call-update) | async-done | bytes 262160 | tf_op jit(solution)/shard_map/psum | solution.py:91
  2001.7 149.7 %all-gather.39.cloned.1.call-done = f32[16384,256]{0,1:T(8,128)} async-done(((f32[2048,256]{0,1:T(8,128)}), f32[16384,256]{0,1:T(8,128)}) %all-gather.39.cloned.1.call-update) | async-done | bytes 16777232 | tf_op jit(solution)/shard_map/all_gather | solution.py:16
  2151.4 18.0 copy.81
  2177.0 125.2 %all-gather.37.cloned.1.call-done = f32[16384,256]{0,1:T(8,128)} async-done(((f32[2048,256]{0,1:T(8,128)}), f32[16384,256]{0,1:T(8,128)}) %all-gather.37.cloned.1.call-update) | async-done | bytes 16777232 | tf_op jit(solution)/shard_map/all_gather | solution.py:16
  2302.2 17.6 copy.79
  2334.4 61.0 %convolution_subtract_fusion = f32[2048,4096]{0,1:T(8,128)} fusion(f32[2048,4096]{0,1:T(8,128)} %convolution_subtract_fusion.1, f32[256,4096]{0,1:T(8,128)} %bitcast.349, f32[256,4096]{0,1:T(8,128)} %bitcast.351, f32[2048,256]{0,1:T(8,128)} %get-tuple-element.142, f32[2048,256]{0,1:T(8,128)S(1)} %get-tuple-element.138), kind=kOutput, calls=%fused_computation.16 | convolution fusion | flops 51551141888 | bytes 79691776 | tf_op jit(solution)/shard_map/dot_general | solution.py:23
  2395.3 31.1 %copy.56 = f32[2048,4096]{1,0:T(8,128)} copy(f32[2048,4096]{0,1:T(8,128)} %convolution_subtract_fusion) | data formatting | bytes 67108864 | tf_op jit(solution)/shard_map/sub | solution.py:95
  (246 shorter events, 244.4 us)
Async XLA Ops:
  6.5 126.9 %all-gather.21.cloned.1.call-start = ((), (), s32[]{:S(2)}) async-start(), calls=%async_computation.4 | async-start | bytes 10485760 | tf_op jit(solution)/shard_map/all_gather | solution.py:16
  43.1 170.1 %all-reduce.20.cloned.1.call-start = ((), (), s32[]{:S(2)}) async-start(), calls=%async_computation.15 | async-start | bytes 1048576 | tf_op jit(solution)/shard_map/psum | solution.py:80
  153.1 2.6 copy-start.2
  156.5 289.1 %all-gather.23.cloned.1.call-start = ((), (), s32[]{:S(2)}) async-start(), calls=%async_computation.5 | async-start | bytes 18874368 | tf_op jit(solution)/shard_map/all_gather | solution.py:16
  275.8 3.7 copy-start.8
  295.2 301.1 %all-gather.25.cloned.1.call-start = ((), (), s32[]{:S(2)}) async-start(), calls=%async_computation.6 | async-start | bytes 18874368 | tf_op jit(solution)/shard_map/all_gather | solution.py:16
  295.8 458.9 %all-reduce.10.cloned.1.call-start = ((), (), s32[]{:S(2)}) async-start(), calls=%async_computation | async-start | bytes 4194304 | tf_op jit(solution)/shard_map/psum | solution.py:89
  626.2 2.0 copy-start
  686.7 131.1 %all-reduce.12.cloned.1.call-start = ((), (), s32[]{:S(2)}) async-start(), calls=%async_computation.1 | async-start | bytes 524288 | tf_op jit(solution)/shard_map/psum | solution.py:91
  758.3 1.4 copy-start.5
  762.2 213.8 %all-gather.27.cloned.1.call-start = ((), (), s32[]{:S(2)}) async-start(), calls=%async_computation.7 | async-start | bytes 18874368 | tf_op jit(solution)/shard_map/all_gather | solution.py:16
  825.8 301.2 %all-gather.29.cloned.1.call-start = ((), (), s32[]{:S(2)}) async-start(), calls=%async_computation.8 | async-start | bytes 18874368 | tf_op jit(solution)/shard_map/all_gather | solution.py:16
  826.5 482.8 %all-gather.31.cloned.1.call-start = ((), (), s32[]{:S(2)}) async-start(), calls=%async_computation.9 | async-start | bytes 10485760 | tf_op jit(solution)/shard_map/all_gather | solution.py:16
  1150.2 1.6 copy-start.6
  1223.5 166.0 %all-reduce.18.cloned.1.call-start = ((), (), s32[]{:S(2)}) async-start(), calls=%async_computation.14 | async-start | bytes 1048576 | tf_op jit(solution)/shard_map/psum | solution.py:80
  1329.4 2.6 copy-start.3
  1332.8 289.6 %all-gather.33.cloned.1.call-start = ((), (), s32[]{:S(2)}) async-start(), calls=%async_computation.10 | async-start | bytes 18874368 | tf_op jit(solution)/shard_map/all_gather | solution.py:16
  1452.9 3.7 copy-start.9
  1472.0 301.1 %all-gather.35.cloned.1.call-start = ((), (), s32[]{:S(2)}) async-start(), calls=%async_computation.11 | async-start | bytes 18874368 | tf_op jit(solution)/shard_map/all_gather | solution.py:16
  1472.6 457.5 %all-reduce.14.cloned.1.call-start = ((), (), s32[]{:S(2)}) async-start(), calls=%async_computation.2 | async-start | bytes 4194304 | tf_op jit(solution)/shard_map/psum | solution.py:89
  1803.0 2.0 copy-start.1
  1862.2 131.0 %all-reduce.16.cloned.1.call-start = ((), (), s32[]{:S(2)}) async-start(), calls=%async_computation.3 | async-start | bytes 524288 | tf_op jit(solution)/shard_map/psum | solution.py:91
  1933.7 1.3 copy-start.4
  1937.6 213.8 %all-gather.39.cloned.1.call-start = ((), (), s32[]{:S(2)}) async-start(), calls=%async_computation.13 | async-start | bytes 18874368 | tf_op jit(solution)/shard_map/all_gather | solution.py:16
  2001.2 301.0 %all-gather.37.cloned.1.call-start = ((), (), s32[]{:S(2)}) async-start(), calls=%async_computation.12 | async-start | bytes 18874368 | tf_op jit(solution)/shard_map/all_gather | solution.py:16
  2325.3 1.6 copy-start.7
Sparse Core Ops, SparseCore 0:
  43.2 90.1 all-gather.20
  156.6 56.5 all-reduce.19
  295.3 150.1 all-gather.22
  447.0 149.2 all-gather.24
  686.8 67.7 all-reduce.9
  762.4 55.4 all-reduce.11
  825.9 150.1 all-gather.26
  977.7 149.2 all-gather.28
  1223.7 85.6 all-gather.30
  1332.9 56.6 all-reduce.17
  1472.2 150.1 all-gather.32
  1623.9 149.2 all-gather.34
  1862.3 67.7 all-reduce.13
  1937.8 55.4 all-reduce.15
  2001.3 150.1 all-gather.38
  2152.9 149.2 all-gather.36
